TPU v7x, 256 devices: a whole 4x4x8 slice. The times are simulated.
256 devices in a mesh: section: 16 (over x, y), tensor: 16 (over z, core).
Axes of the slice: x: 4, y: 4, z: 8, core: 2. Of those that a mesh axis runs over, the one named last changes fastest.
Arguments:
- queries: bfloat16 [16, 512, 8192], P('section', None, 'tensor'), may hold values from -20 to 20
- key_rows: bfloat16 [16, 512, 1024], P('section'), may hold values from -6 to 6
- value_rows: bfloat16 [16, 512, 1024], P('section'), may hold values from -6 to 6
- out_grad: bfloat16 [16, 512, 8192], P('section', None, 'tensor'), may hold values from -24 to 24
- layer_input: bfloat16 [16, 512, 8192], P('section', 'tensor'), may hold values from -64 to 64
- query_weight: bfloat16 [16, 8192, 8192], P('section', None, 'tensor'), may hold values from -0.0625 to 0.0625
- dion_basis: float32 [16, 8192, 256], P('section', 'tensor'), may hold values from -0.0625 to 0.0625
- lengths: int32 [16, 3], P('section'), may hold values from 1 to 256, 512 in all within a row
Outputs:
- upstream: bfloat16 [16, 512, 8192], P('section', 'tensor')
- left_factor: float32 [16, 8192, 256], P('section', 'tensor')
- right_factor: float32 [16, 8192, 256], P('section', 'tensor')
Inputs may be any that keep to these rules, and one draw needn't show every extreme that they name: For each section the lengths of the prompt, the chosen and the rejected response, in that order, summing to 512.
All inputs are finite; a program needn't handle non-finite values.
Results may differ from a plain program's by a relative error of at most 0.022.
Values may be sent and summed in bfloat16 or wider, within the bound.
No kernel may reach another device: no remote copies, remote signals or barrier semaphores. Data moves between devices by JAX's collectives and lax.ppermute only.
A program may use at most 64 MiB of HBM per device.

v0:
```python
import math
import jax
import jax.numpy as jnp
from jax import lax
from jax.sharding import PartitionSpec as P

D = 8192
HD = 128
GROUP = 8
rope_base = 500000.0
highest = lax.Precision.HIGHEST


def shifted(value, axis, steps):
    count = lax.axis_size(axis)
    first, last = (max(0, -steps), min(count, count - steps))
    return lax.ppermute(value, axis, [(source, source + steps) for source in range(first, last)])


def tree_layout(lengths_row, token_count):
    token_ids = jnp.arange(token_count, dtype=jnp.int32)
    bound_one = lengths_row[0]
    bound_two = lengths_row[0] + lengths_row[1]
    positions = jnp.where(token_ids < bound_two, token_ids, token_ids - lengths_row[1]).astype(
        jnp.float32
    )
    row_ids = token_ids[:, None]
    col_ids = token_ids[None, :]
    crossed = (row_ids >= bound_two) & (col_ids >= bound_one) & (col_ids < bound_two)
    visible = (col_ids <= row_ids) & jnp.logical_not(crossed)
    return (positions, visible)


def unrotate(rotated, positions):
    head_dim = rotated.shape[-1]
    half_dim = head_dim // 2
    freq_ids = jnp.arange(half_dim, dtype=jnp.float32)
    inverse = jnp.exp(-math.log(rope_base) * 2.0 * freq_ids / head_dim)
    angles = positions[:, None] * inverse[None, :]
    cosine = jnp.cos(angles)[:, None, :]
    sine_part = jnp.sin(angles)[:, None, :]
    first_half = rotated[..., :half_dim]
    second_half = rotated[..., half_dim:]
    return jnp.concatenate(
        [
            first_half * cosine + second_half * sine_part,
            second_half * cosine - first_half * sine_part,
        ],
        axis=-1,
    )


def local_backward(query_heads, grad_heads, key_block, value_block, visible):
    score_scale = 1.0 / math.sqrt(query_heads.shape[-1])
    scores = (
        jnp.einsum("qhd,kd->hqk", query_heads, key_block, preferred_element_type=jnp.float32)
        * score_scale
    )
    scores = jnp.where(visible[None], scores, -jnp.inf)
    row_max = jnp.max(scores, axis=-1, keepdims=True)
    exp_scores = jnp.exp(scores - row_max)
    weights = exp_scores / jnp.sum(exp_scores, axis=-1, keepdims=True)
    weights_low = weights.astype(jnp.bfloat16)
    outputs = jnp.einsum(
        "hqk,kd->qhd", weights_low, value_block, preferred_element_type=jnp.float32
    )
    out_dot = jnp.sum(grad_heads.astype(jnp.float32) * outputs, axis=-1)
    prob_grad = jnp.einsum(
        "qhd,kd->hqk", grad_heads, value_block, preferred_element_type=jnp.float32
    )
    score_grad = (weights * (prob_grad - out_dot.T[:, :, None])).astype(jnp.bfloat16)
    return (
        jnp.einsum("hqk,kd->qhd", score_grad, key_block, preferred_element_type=jnp.float32)
        * score_scale
    )


def local(queries, key_rows, value_rows, out_grad, layer_input, query_weight, dion_basis, lengths):
    token_count = queries.shape[1]
    local_width = queries.shape[2]
    local_heads = local_width // HD
    tensor_count = lax.axis_size("tensor")
    tensor_index = lax.axis_index("tensor")
    col_width = D // tensor_count
    gathered = lax.all_gather(layer_input[0], "tensor", axis=0, tiled=True)
    columns = lax.dynamic_slice_in_dim(gathered, tensor_index * col_width, col_width, 1)
    positions, visible = tree_layout(lengths[0], token_count)
    group_head = tensor_index * local_heads // GROUP
    key_block = lax.dynamic_slice_in_dim(key_rows[0], group_head * HD, HD, 1)
    value_block = lax.dynamic_slice_in_dim(value_rows[0], group_head * HD, HD, 1)
    rotated = local_backward(
        queries[0].reshape(token_count, local_heads, HD),
        out_grad[0].reshape(token_count, local_heads, HD),
        key_block,
        value_block,
        visible,
    )
    query_grad = unrotate(rotated, positions).reshape(token_count, local_width).astype(jnp.bfloat16)
    weight_local = query_weight[0]
    layer_grad = lax.psum_scatter(
        lax.dot_general(
            query_grad, weight_local, (((1,), (1,)), ((), ())), preferred_element_type=jnp.float32
        ).astype(jnp.bfloat16),
        "tensor",
        scatter_dimension=0,
        tiled=True,
    )
    upstream = shifted(layer_grad, "section", -1)
    grad_wide = query_grad.astype(jnp.float32)
    projected = lax.psum(jnp.dot(grad_wide, dion_basis[0], precision=highest), "tensor")
    column_wide = columns.astype(jnp.float32)
    left_raw = lax.dot_general(column_wide, projected, (((0,), (0,)), ((), ())), precision=highest)
    gram_part = lax.dot_general(left_raw, left_raw, (((0,), (0,)), ((), ())), precision=highest)
    mixed_part = jnp.dot(column_wide, left_raw, precision=highest)
    gram_total, mixed_total = lax.psum((gram_part, mixed_part), "tensor")
    lower_factor = jnp.linalg.cholesky(gram_total)
    left_orth = lax.linalg.triangular_solve(
        lower_factor, left_raw, left_side=False, lower=True, transpose_a=True
    )
    mixed_orth = lax.linalg.triangular_solve(
        lower_factor, mixed_total, left_side=False, lower=True, transpose_a=True
    )
    right_factor = lax.dot_general(
        grad_wide, mixed_orth, (((0,), (0,)), ((), ())), precision=highest
    )
    return (upstream[None], (left_orth * math.sqrt(D))[None], right_factor[None])


def solution(mesh):
    placed = (
        P("section", None, "tensor"),
        P("section", None, None),
        P("section", None, None),
        P("section", None, "tensor"),
        P("section", "tensor", None),
        P("section", None, "tensor"),
        P("section", "tensor", None),
        P("section", None),
    )
    return jax.shard_map(
        local,
        mesh=mesh,
        in_specs=placed,
        out_specs=(
            P("section", "tensor", None),
            P("section", "tensor", None),
            P("section", "tensor", None),
        ),
        check_vma=False,
    )
```

profile of v0, /device:TPU:26, one launch (start us, length us, event | category | flops | bytes accessed | tf_op | source)
XLA Modules:
  0.0 409.4 jit_solution(8106175779800506039)
XLA Ops:
  7.2 1.3 fusion.63
  11.2 1.2 reshape_squeeze.6
  12.4 0.7 fusion.27
  13.4 2.1 fusion.64
  15.5 1.9 copy-done.3
  17.4 1.4 fusion.5
  19.2 1.2 reshape_squeeze.7
  21.1 3.5 fusion.12
  25.4 1.5 fusion.19
  27.0 0.7 all-gather.3.cloned.1.call-update
  27.7 111.7 %all-reduce.5.cloned.1.call-done = f32[512,256]{1,0:T(8,128)} async-done(((f32[512,256]{1,0:T(8,128)}), f32[512,256]{1,0:T(8,128)}) %all-reduce.5.cloned.1.call-update) | async-done | bytes 524304 | tf_op jit(solution)/shard_map/psum | solution.py:110
  139.4 58.2 %all-gather.3.cloned.1.call-done = bf16[1,512,8192]{2,1,0:T(8,128)(2,1)} async-done(((bf16[1,32,8192]{2,1,0:T(8,128)(2,1)}), bf16[1,512,8192]{2,1,0:T(8,128)(2,1)}) %all-gather.3.cloned.1.call-update) | async-done | bytes 8388624 | tf_op jit(solution)/shard_map/all_gather | solution.py:85
  197.7 1.9 fusion.23
  199.6 1.7 fusion.65
  201.3 2.5 fusion.21
  203.9 10.2 %convolution_convert_fusion = bf16[512,8192]{1,0:T(8,128)(2,1)} fusion(bf16[512,512]{0,1:T(8,128)(2,1)S(1)} %bitcast.114, bf16[1,8192,512]{2,1,0:T(8,128)(2,1)} %param.15), kind=kOutput, calls=%fused_computation.3 | convolution fusion | flops 4299161600 | bytes 17301504 | tf_op jit(solution)/shard_map/dot_general | solution.py:101
  214.1 99.1 %all-reduce.7.cloned.1.call-done = (f32[256,256]{0,1:T(8,128)}, f32[512,256]{1,0:T(8,128)}) async-done(((f32[256,256]{0,1:T(8,128)}, f32[512,256]{1,0:T(8,128)}), (f32[256,256]{0,1:T(8,128)}, f32[512,256]{1,0:T(8,128)})) %all-reduce.7.cloned.1.call-update) | async-done | bytes 786448 | tf_op jit(solution)/shard_map/psum | solution.py:115
  313.3 1.1 copy.22
  314.4 1.0 fusion.35
  315.4 11.7 %cholesky.50 = f32[128,128]{1,0:T(8,128)S(1)} custom-call(f32[128,128]{1,0:T(8,128)S(1)} %cholesky.118), custom_call_target="Cholesky" | custom-call | tf_op jit(solution)/shard_map/jit(cholesky)/cholesky | solution.py:116
  327.2 9.8 %custom-call.14 = f32[1,128,128]{1,2,0:T(8,128)S(1)} custom-call(f32[1,128,128]{2,1,0:T(8,128)S(1)} %get-tuple-element.43), custom_call_target="InvertDiagBlocksLowerTriangular" | custom-call | tf_op jit(solution)/shard_map/jit(cholesky)/cholesky | solution.py:116
  337.5 11.7 %cholesky.105 = f32[128,128]{1,0:T(8,128)S(1)} custom-call(f32[128,128]{1,0:T(8,128)S(1)} %convolution_subtract_fusion.2), custom_call_target="Cholesky" | custom-call | tf_op jit(solution)/shard_map/jit(cholesky)/cholesky | solution.py:116
  351.9 4.0 while.4
  352.5 1.4 bitcast_dynamic-update-slice_fusion.2
  354.5 1.4 bitcast_dynamic-update-slice_fusion.2
  355.9 19.9 %custom-call.16 = f32[2,128,128]{1,2,0:T(8,128)S(1)} custom-call(f32[2,128,128]{2,1,0:T(8,128)S(1)} %get-tuple-element.18), custom_call_target="InvertDiagBlocksLowerTriangular" | custom-call | tf_op jit(solution)/shard_map/triangular_solve/custom-call.0 | solution.py:117
  377.3 1.0 copy.23
  378.8 8.2 %reduce-scatter.2.cloned.1.call-done = bf16[32,8192]{1,0:T(8,128)(2,1)} async-done(((bf16[512,8192]{1,0:T(8,128)(2,1)}), bf16[32,8192]{1,0:T(8,128)(2,1)}) %reduce-scatter.2.cloned.1.call-update) | async-done | bytes 524304 | tf_op jit(solution)/shard_map/reduce_scatter | solution.py:100
  387.0 2.8 collective-permute-start
  390.8 1.4 convolution_bitcast_fusion
  392.2 9.8 %collective-permute-done = bf16[32,8192]{1,0:T(8,128)(2,1)S(1)} collective-permute-done((bf16[32,8192]{1,0:T(8,128)(2,1)}, bf16[32,8192]{1,0:T(8,128)(2,1)S(1)}, u32[]{:S(2)}, u32[]{:S(2)}) %collective-permute-start) | collective-permute-done | bytes 524320 | tf_op jit(solution)/shard_map/ppermute | solution.py:17
  402.1 0.8 copy.50
  (48 shorter events, 9.6 us)
Async XLA Ops:
  7.2 5.2 %copy-start = (bf16[1,512,1024]{2,1,0:T(8,128)(2,1)S(1)}, bf16[1,512,1024]{2,1,0:T(8,128)(2,1)}, u32[]{:S(2)}) copy-start(bf16[1,512,1024]{2,1,0:T(8,128)(2,1)} %param.11) | copy-start | bytes 3145732
  7.2 132.2 %all-reduce.5.cloned.1.call-start = ((), (), s32[]{:S(2)}) async-start(), calls=%async_computation.2 | async-start | bytes 1048576 | tf_op jit(solution)/shard_map/psum | solution.py:110
  15.5 1.9 copy-start.3
  21.1 4.2 %copy-start.1 = (f32[1,512,256]{2,1,0:T(8,128)S(1)}, f32[1,512,256]{2,1,0:T(8,128)}, u32[]{:S(2)}) copy-start(f32[1,512,256]{2,1,0:T(8,128)} %param.16) | copy-start | bytes 1572868
  26.9 170.7 %all-gather.3.cloned.1.call-start = ((), (), s32[]{:S(2)}) async-start(), calls=%async_computation.3 | async-start | bytes 8912896 | tf_op jit(solution)/shard_map/all_gather | solution.py:85
  27.7 285.6 %all-reduce.7.cloned.1.call-start = ((), (), s32[]{:S(2)}) async-start(), calls=%async_computation.4 | async-start | bytes 1572864 | tf_op jit(solution)/shard_map/psum | solution.py:115
  203.8 183.2 %reduce-scatter.2.cloned.1.call-start = ((), (), s32[]{:S(2)}) async-start(), calls=%async_computation.1 | async-start | bytes 8912896 | tf_op jit(solution)/shard_map/reduce_scatter | solution.py:100
  313.3 65.1 %copy-start.2 = (f32[512,256]{1,0:T(8,128)S(1)}, f32[512,256]{1,0:T(8,128)}, u32[]{:S(2)}) copy-start(f32[512,256]{1,0:T(8,128)} %get-tuple-element.35) | copy-start | bytes 1572868
  387.0 15.1 %collective-permute-start = (bf16[32,8192]{1,0:T(8,128)(2,1)}, bf16[32,8192]{1,0:T(8,128)(2,1)S(1)}, u32[]{:S(2)}, u32[]{:S(2)}) collective-permute-start(bf16[32,8192]{1,0:T(8,128)(2,1)} %reduce-scatter.2.cloned.1.call-done), channel_id=1, source_target_pairs={{16,0},{32,16},{48,32},{64,48},{80,64},{96,80},{112,96},{128,112},... | collective-permute-start | bytes 1572872 | tf_op jit(solution)/shard_map/ppermute | solution.py:17
Sparse Core Ops, SparseCore 0:
  27.1 112.3 all-reduce.4
  141.4 56.2 all-gather.2
  203.9 109.2 all-reduce.6
  315.7 71.2 reduce-scatter.1
where the time goes:
time: 410 us; the launch traced here: 409 us
  waiting for transfers between devices  288 us (70%)
  other arithmetic  60.6 us (15%)
  matrix products  28.2 us (7%)
  between operations  16.7 us (4%)
  local copies, waits for them, and re-layouts  13.1 us (3%)
    psum x1, waiting for transfers between devices, local(): lax.psum(jnp.dot(grad_wide, dion_basis[0], precision=highest), 'tensor')  112 us
    psum x1, waiting for transfers between devices, local(): gram_total, mixed_total = lax.psum((gram_part, mixed_part), 'tensor')  99.1 us
    all_gather x1, waiting for transfers between devices, local(): gathered = lax.all_gather(layer_input[0], 'tensor', axis=0, tiled=True)  58.2 us
    another operation x7, other arithmetic, local(): lower_factor = jnp.linalg.cholesky(gram_total)  34.6 us
    another operation x4, other arithmetic, local(): lax.linalg.triangular_solve(lower_factor, left_raw, left_side=False, lowe...  19.9 us
    dot_general x1, matrix products, local(): lax.dot_general(query_grad, weight_local, (((1,), (1,)), ((), ())), prefe...  10.2 us
    ppermute x1, waiting for transfers between devices, shifted(): lax.ppermute(value, axis, [(source, source + steps) for source in range(f...  9.81 us
    reduce_scatter x1, waiting for transfers between devices, local(): lax.psum_scatter(lax.dot_general(query_grad, weight_local, (((1,), (1,)),...  8.25 us
  transfers between devices with their start and end apart: 5, of which 5 were waited for; matrix products, arithmetic and copies ran while one was open for 19% of the time, Pallas kernels for 0%

commit v1 on v0

--- a/solution.py
+++ b/solution.py
@@ -82,7 +82,10 @@
     tensor_count = lax.axis_size("tensor")
     tensor_index = lax.axis_index("tensor")
     col_width = D // tensor_count
-    gathered = lax.all_gather(layer_input[0], "tensor", axis=0, tiled=True)
+    gathered = jnp.concatenate(
+        lax.all_to_all(jnp.stack([layer_input[0]] * lax.axis_size("tensor")), "tensor", 0, 0),
+        axis=0,
+    )
     columns = lax.dynamic_slice_in_dim(gathered, tensor_index * col_width, col_width, 1)
     positions, visible = tree_layout(lengths[0], token_count)
     group_head = tensor_index * local_heads // GROUP

time: 410 us -> 445 us (1.085)
  waiting for transfers between devices: 288 us -> 311 us
  starting transfers between devices: 2.95 us -> 11.3 us
    psum x1, waiting for transfers between devices: 112 us -> 192 us  [local(): lax.psum(jnp.dot(grad_wide, dion_basis[0], precision=highest), 'tensor')]
    all_gather x1 -> x0, waiting for transfers between devices: 58.2 us -> none  [local(): gathered = lax.all_gather(layer_input[0], 'tensor', axis=0, tiled=True)]
    all_to_all x0 -> x1, starting transfers between devices: none -> 8.75 us  [local(): lax.all_to_all(jnp.stack([layer_input[0]] * lax.axis_size('tensor')), 'te...]
    another operation x0 -> x1, local copies, waits for them, and re-layouts: none -> 5.38 us  [local(): jnp.stack([layer_input[0]] * lax.axis_size('tensor'))]
  transfers between devices with their start and end apart: 5 -> 5, of which waited for: 5 -> 4; matrix products, arithmetic and copies ran while one was open for 19% -> 21% of each run, Pallas kernels for 0% -> 0%
where the time goes in v1:
time: 445 us; the launch traced here: 444 us
  waiting for transfers between devices  311 us (70%)
  other arithmetic  60.6 us (14%)
  matrix products  28.2 us (6%)
  local copies, waits for them, and re-layouts  16.7 us (4%)
  between operations  16.7 us (4%)
  starting transfers between devices  11.3 us (3%)
    psum x1, waiting for transfers between devices, local(): lax.psum(jnp.dot(grad_wide, dion_basis[0], precision=highest), 'tensor')  192 us
    psum x1, waiting for transfers between devices, local(): gram_total, mixed_total = lax.psum((gram_part, mixed_part), 'tensor')  101 us
    another operation x7, other arithmetic, local(): lower_factor = jnp.linalg.cholesky(gram_total)  34.6 us
    another operation x4, other arithmetic, local(): lax.linalg.triangular_solve(lower_factor, left_raw, left_side=False, lowe...  19.9 us
    dot_general x1, matrix products, local(): lax.dot_general(query_grad, weight_local, (((1,), (1,)), ((), ())), prefe...  10.2 us
    ppermute x1, waiting for transfers between devices, shifted(): lax.ppermute(value, axis, [(source, source + steps) for source in range(f...  10 us
  transfers between devices with their start and end apart: 5, of which 4 were waited for; matrix products, arithmetic and copies ran while one was open for 21% of the time, Pallas kernels for 0%

profile of v1, /device:TPU:26, one launch (start us, length us, event | category | flops | bytes accessed | tf_op | source)
XLA Modules:
  0.0 444.4 jit_solution(4569880823112886271)
XLA Ops:
  7.2 5.4 %stack.3 = bf16[16,32,8192]{2,1,0:T(8,128)(2,1)} broadcast(bf16[32,8192]{1,0:T(8,128)(2,1)} %bitcast.116), dimensions={1,2} | broadcast | bytes 8912896 | tf_op jit(solution)/shard_map/stack | solution.py:86
  12.6 8.8 %all-to-all-start = ((bf16[16,32,8192]{2,1,0:T(8,128)(2,1)}), bf16[16,32,8192]{2,1,0:T(8,128)(2,1)}, u32[]{:S(2)}, u32[]{:S(2)}) async-start(bf16[16,32,8192]{2,1,0:T(8,128)(2,1)} %stack.3), calls=%async_computation.1 | async-start | bytes 16777216 | tf_op jit(solution)/shard_map/all_to_all | solution.py:86
  23.4 0.7 iota_compare_fusion.5
  24.4 0.7 fusion.23
  25.1 2.1 fusion.62
  27.2 1.9 copy-done.5
  29.2 1.4 fusion.5
  30.9 1.2 reshape_squeeze.7
  32.9 0.7 select_convert_fusion
  34.1 3.5 fusion.12
  37.8 1.5 fusion.19
  39.4 191.8 %all-reduce.5.cloned.1.call-done = f32[512,256]{1,0:T(8,128)} async-done(((f32[512,256]{1,0:T(8,128)}), f32[512,256]{1,0:T(8,128)}) %all-reduce.5.cloned.1.call-update) | async-done | bytes 524304 | tf_op jit(solution)/shard_map/psum | solution.py:113
  231.2 1.9 fusion.27
  233.1 2.5 fusion.25
  235.6 1.7 fusion.63
  237.4 10.2 %convolution_convert_fusion = bf16[512,8192]{1,0:T(8,128)(2,1)} fusion(bf16[512,512]{0,1:T(8,128)(2,1)S(1)} %bitcast.111, bf16[1,8192,512]{2,1,0:T(8,128)(2,1)} %param.15), kind=kOutput, calls=%fused_computation.3 | convolution fusion | flops 4299161600 | bytes 17301504 | tf_op jit(solution)/shard_map/dot_general | solution.py:104
  247.7 100.5 %all-reduce.7.cloned.1.call-done = (f32[256,256]{0,1:T(8,128)}, f32[512,256]{1,0:T(8,128)}) async-done(((f32[256,256]{0,1:T(8,128)}, f32[512,256]{1,0:T(8,128)}), (f32[256,256]{0,1:T(8,128)}, f32[512,256]{1,0:T(8,128)})) %all-reduce.7.cloned.1.call-update) | async-done | bytes 786448 | tf_op jit(solution)/shard_map/psum | solution.py:118
  348.2 1.1 copy.22
  349.3 1.0 fusion.33
  350.3 11.7 %cholesky.50 = f32[128,128]{1,0:T(8,128)S(1)} custom-call(f32[128,128]{1,0:T(8,128)S(1)} %cholesky.118), custom_call_target="Cholesky" | custom-call | tf_op jit(solution)/shard_map/jit(cholesky)/cholesky | solution.py:119
  362.1 9.8 %custom-call.14 = f32[1,128,128]{1,2,0:T(8,128)S(1)} custom-call(f32[1,128,128]{2,1,0:T(8,128)S(1)} %get-tuple-element.43), custom_call_target="InvertDiagBlocksLowerTriangular" | custom-call | tf_op jit(solution)/shard_map/jit(cholesky)/cholesky | solution.py:119
  372.4 11.7 %cholesky.105 = f32[128,128]{1,0:T(8,128)S(1)} custom-call(f32[128,128]{1,0:T(8,128)S(1)} %convolution_subtract_fusion.2), custom_call_target="Cholesky" | custom-call | tf_op jit(solution)/shard_map/jit(cholesky)/cholesky | solution.py:119
  386.9 4.0 while.4
  387.4 1.4 bitcast_dynamic-update-slice_fusion.2
  389.4 1.4 bitcast_dynamic-update-slice_fusion.2
  390.8 19.9 %custom-call.16 = f32[2,128,128]{1,2,0:T(8,128)S(1)} custom-call(f32[2,128,128]{2,1,0:T(8,128)S(1)} %get-tuple-element.18), custom_call_target="InvertDiagBlocksLowerTriangular" | custom-call | tf_op jit(solution)/shard_map/triangular_solve/custom-call.0 | solution.py:120
  412.3 1.0 copy.23
  413.7 8.5 %reduce-scatter.2.cloned.1.call-done = bf16[32,8192]{1,0:T(8,128)(2,1)} async-done(((bf16[512,8192]{1,0:T(8,128)(2,1)}), bf16[32,8192]{1,0:T(8,128)(2,1)}) %reduce-scatter.2.cloned.1.call-update) | async-done | bytes 524304 | tf_op jit(solution)/shard_map/reduce_scatter | solution.py:103
  422.2 2.5 collective-permute-start
  425.6 1.4 convolution_bitcast_fusion
  427.1 10.0 %collective-permute-done = bf16[32,8192]{1,0:T(8,128)(2,1)S(1)} collective-permute-done((bf16[32,8192]{1,0:T(8,128)(2,1)}, bf16[32,8192]{1,0:T(8,128)(2,1)S(1)}, u32[]{:S(2)}, u32[]{:S(2)}) %collective-permute-start) | collective-permute-done | bytes 524320 | tf_op jit(solution)/shard_map/ppermute | solution.py:17
  437.1 0.8 copy.50
  (52 shorter events, 9.0 us)
Async XLA Ops:
  7.2 17.2 %copy-start = (bf16[1,512,1024]{2,1,0:T(8,128)(2,1)S(1)}, bf16[1,512,1024]{2,1,0:T(8,128)(2,1)}, u32[]{:S(2)}) copy-start(bf16[1,512,1024]{2,1,0:T(8,128)(2,1)} %param.11) | copy-start | bytes 3145732
  12.6 8.8 %copy-start.2 = (bf16[1,512,512]{2,1,0:T(8,128)(2,1)S(1)}, bf16[1,512,512]{2,1,0:T(8,128)(2,1)}, u32[]{:S(2)}) copy-start(bf16[1,512,512]{2,1,0:T(8,128)(2,1)} %param.10) | copy-start | bytes 1572868
  12.6 9.0 %copy-start.4 = (s32[1,3]{1,0:T(1,128)S(1)}, s32[1,3]{1,0:T(1,128)}, u32[]{:S(2)}) copy-start(s32[1,3]{1,0:T(1,128)} %param.17) | copy-start | bytes 40
  12.6 218.6 %all-to-all-start = ((bf16[16,32,8192]{2,1,0:T(8,128)(2,1)}), bf16[16,32,8192]{2,1,0:T(8,128)(2,1)}, u32[]{:S(2)}, u32[]{:S(2)}) async-start(bf16[16,32,8192]{2,1,0:T(8,128)(2,1)} %stack.3), calls=%async_computation.1 | async-start | bytes 16777216 | tf_op jit(solution)/shard_map/all_to_all | solution.py:86
  21.3 209.9 %all-reduce.5.cloned.1.call-start = ((), (), s32[]{:S(2)}) async-start(), calls=%async_computation.3 | async-start | bytes 1048576 | tf_op jit(solution)/shard_map/psum | solution.py:113
  27.2 1.9 copy-start.5
  34.1 3.7 copy-start.1
  39.3 308.9 %all-reduce.7.cloned.1.call-start = ((), (), s32[]{:S(2)}) async-start(), calls=%async_computation.4 | async-start | bytes 1572864 | tf_op jit(solution)/shard_map/psum | solution.py:118
  237.3 184.8 %reduce-scatter.2.cloned.1.call-start = ((), (), s32[]{:S(2)}) async-start(), calls=%async_computation.2 | async-start | bytes 8912896 | tf_op jit(solution)/shard_map/reduce_scatter | solution.py:103
  348.2 65.1 %copy-start.3 = (f32[512,256]{1,0:T(8,128)S(1)}, f32[512,256]{1,0:T(8,128)}, u32[]{:S(2)}) copy-start(f32[512,256]{1,0:T(8,128)} %get-tuple-element.35) | copy-start | bytes 1572868
  422.2 14.9 %collective-permute-start = (bf16[32,8192]{1,0:T(8,128)(2,1)}, bf16[32,8192]{1,0:T(8,128)(2,1)S(1)}, u32[]{:S(2)}, u32[]{:S(2)}) collective-permute-start(bf16[32,8192]{1,0:T(8,128)(2,1)} %reduce-scatter.2.cloned.1.call-done), channel_id=1, source_target_pairs={{16,0},{32,16},{48,32},{64,48},{80,64},{96,80},{112,96},{128,112},... | collective-permute-start | bytes 1572872 | tf_op jit(solution)/shard_map/ppermute | solution.py:17
Sparse Core Ops, SparseCore 0:
  39.5 191.6 all-reduce.4
  237.5 110.6 all-reduce.6
  350.8 71.3 reduce-scatter.1
